TPU v7x, 128 devices: a whole 4x4x4 slice. The times are simulated.
128 devices in a mesh: val: 4 (over x_hi, core), cond: 8 (over z, x_lo), grid: 4 (over y).
Axes of the slice: x: 4 (x_hi: 2, x_lo: 2; x = x_hi * 2 + x_lo), y: 4, z: 4, core: 2. Of those that a mesh axis runs over, the one named last changes fastest.
Arguments:
- valence_orbitals: bfloat16 [16, 96, 9216], P('val', 'grid'), may hold values from -6 to 6
- conduction_orbitals: bfloat16 [32, 96, 9216], P('cond', 'grid'), may hold values from -6 to 6
- valence_energy: float32 [16], replicated, may hold values from -12 to -1
- conduction_energy: float32 [32], replicated, may hold values from 0.5 to 10
- grid_index: int32 [6144], replicated, may hold values from 0 to 884735, as said below
Outputs:
- response: float32 [2, 6144, 6144], P(None, ('val', 'grid'), 'cond')
Inputs may be any that keep to these rules, and one draw needn't show every extreme that they name: `grid_index`: distinct flat points of the 96 x 96 x 96 frequency grid.
All inputs are finite; a program needn't handle non-finite values.
Results may differ from a plain program's by a relative error of at most 0.0098.
Values may be sent and summed in bfloat16 or wider, within the bound.
No kernel may reach another device: no remote copies, remote signals or barrier semaphores. Data moves between devices by JAX's collectives and lax.ppermute only.
A program may use at most 128 MiB of HBM per device.

v0:
```python
import math
import jax
import jax.numpy as jnp
from jax import lax
from jax.sharding import PartitionSpec as P

NGRID = 96
NG = 6144
freq_squared = 4.0


def line_tables(points):
    indices = jnp.arange(points, dtype=jnp.int32)
    phases = indices[:, None] * indices[None, :] % points
    angles = phases.astype(jnp.float32) * (2.0 * math.pi / points)
    return (jnp.cos(angles).astype(jnp.bfloat16), (-jnp.sin(angles)).astype(jnp.bfloat16))


def plane_pass(products):
    line_cos, line_sin = line_tables(NGRID)
    z_table = jnp.concatenate([line_cos, line_sin], axis=1)
    row_total = products.shape[0]
    z_part = jnp.dot(
        products.reshape(row_total * NGRID, NGRID), z_table, preferred_element_type=jnp.float32
    )
    z_part = z_part.astype(jnp.bfloat16).reshape(row_total, NGRID, 2 * NGRID)
    first = jnp.einsum("ryk,yp->rpk", z_part, line_cos, preferred_element_type=jnp.float32)
    second = jnp.einsum("ryk,yp->rpk", z_part, line_sin, preferred_element_type=jnp.float32)
    plane_real = first[..., :NGRID] - second[..., NGRID:]
    plane_imag = second[..., :NGRID] + first[..., NGRID:]
    return jnp.concatenate([plane_real, plane_imag], axis=-1).astype(jnp.bfloat16)


def band_spectra(orbital, conduction_part):
    products = (orbital.astype(jnp.float32)[None] * conduction_part.astype(jnp.float32)).astype(
        jnp.bfloat16
    )
    band_total = conduction_part.shape[0]
    depth = conduction_part.shape[1]
    spectra = plane_pass(products.reshape(band_total * depth, NGRID, NGRID))
    return spectra.reshape(band_total, depth, NGRID, 2 * NGRID)


def line_pick(pieces, grid_index, row_offset):
    line_cos, line_sin = line_tables(NGRID)
    pair_total = pieces.shape[0]
    local_rows = pieces.shape[2]
    split = pieces.reshape(pair_total, NGRID, local_rows, 2, NGRID)
    table_rows = jnp.transpose(split, (2, 4, 1, 0, 3)).reshape(
        local_rows * NGRID, NGRID, pair_total * 2
    )
    plane_size = NGRID * NGRID
    vector_total = grid_index.shape[0]
    line_number = grid_index // plane_size
    remainder = grid_index % plane_size
    local_row = remainder // NGRID - row_offset
    column = remainder % NGRID
    inside = (local_row >= 0) & (local_row < local_rows)
    row_index = jnp.clip(local_row, 0, local_rows - 1) * NGRID + column
    block = math.gcd(vector_total, 512)
    count = vector_total // block
    scale = NGRID ** (-1.5)
    factor = jnp.where(inside, scale, 0.0).astype(jnp.float32)
    frequencies = jnp.arange(NGRID, dtype=jnp.int32)

    def one_block(item):
        lines, picks, keep = item
        picked = jnp.take(table_rows, picks, axis=0).reshape(block, NGRID, pair_total, 2)
        onehot = (lines[:, None] == frequencies[None, :]).astype(jnp.bfloat16)
        cos_pick = jnp.dot(onehot, line_cos.T, preferred_element_type=jnp.float32).astype(
            jnp.bfloat16
        )
        sin_pick = jnp.dot(onehot, line_sin.T, preferred_element_type=jnp.float32).astype(
            jnp.bfloat16
        )
        real_part = picked[..., 0]
        imag_part = picked[..., 1]
        real_out = jnp.einsum(
            "jx,jxp->jp", cos_pick, real_part, preferred_element_type=jnp.float32
        ) - jnp.einsum("jx,jxp->jp", sin_pick, imag_part, preferred_element_type=jnp.float32)
        imag_out = jnp.einsum(
            "jx,jxp->jp", sin_pick, real_part, preferred_element_type=jnp.float32
        ) + jnp.einsum("jx,jxp->jp", cos_pick, imag_part, preferred_element_type=jnp.float32)
        return jnp.stack([real_out * keep[:, None], imag_out * keep[:, None]])

    blocks = lax.map(
        one_block,
        (
            line_number.reshape(count, block),
            row_index.reshape(count, block),
            factor.reshape(count, block),
        ),
    )
    result = jnp.transpose(blocks, (1, 3, 0, 2)).reshape(2, pair_total, vector_total)
    return result.astype(jnp.bfloat16)


def local(valence_orbitals, conduction_orbitals, valence_energy, conduction_energy, grid_index):
    valence_groups = lax.axis_size("val")
    conduction_groups = lax.axis_size("cond")
    grid_groups = lax.axis_size("grid")
    valence_local = valence_orbitals.shape[0]
    conduction_local = conduction_orbitals.shape[0]
    pair_count = valence_local * conduction_local
    slab_depth = valence_orbitals.shape[1]

    def one_valence(orbital):
        return band_spectra(orbital, conduction_orbitals)

    spectra = lax.map(one_valence, valence_orbitals)
    spectra = spectra.reshape(pair_count, slab_depth, NGRID, 2 * NGRID)
    row_offset = lax.axis_index("grid") * (NGRID // grid_groups)
    partial_values = line_pick(
        lax.all_to_all(spectra, "grid", split_axis=2, concat_axis=1, tiled=True),
        grid_index,
        row_offset,
    )
    pair_values = lax.psum(partial_values.astype(jnp.float32).astype(jnp.bfloat16), "grid")
    delta = valence_energy[:, None] - conduction_energy[None, :]
    all_pairs = valence_energy.shape[0] * conduction_energy.shape[0]
    weights = 4.0 * delta / (delta * delta + freq_squared) / math.sqrt(all_pairs)
    weights = weights.reshape(valence_groups, valence_local, conduction_groups, conduction_local)
    weights = jnp.transpose(weights, (0, 2, 1, 3)).reshape(all_pairs)
    row_width = NG // (valence_groups * grid_groups)
    split_view = pair_values.reshape(2, pair_count, valence_groups, grid_groups, row_width)
    grid_rows = lax.dynamic_index_in_dim(split_view, lax.axis_index("grid"), 3, keepdims=False)
    everything = lax.all_gather(
        grid_rows.reshape(2, pair_count, valence_groups * row_width),
        ("val", "cond"),
        axis=1,
        tiled=True,
    )
    row_values = lax.dynamic_slice_in_dim(
        everything, lax.axis_index("val") * row_width, row_width, 2
    )
    scaled_rows = (row_values.astype(jnp.float32) * weights[None, :, None]).astype(jnp.bfloat16)
    by_column = lax.all_to_all(pair_values, "cond", split_axis=2, concat_axis=1, tiled=True)
    contract = (((0,), (0,)), ((), ()))
    piece = lax.all_gather(by_column, "val", axis=1, tiled=True)
    real_sum = lax.dot_general(
        scaled_rows[0], piece[0], contract, preferred_element_type=jnp.float32
    )
    real_sum = real_sum + lax.dot_general(
        scaled_rows[1], piece[1], contract, preferred_element_type=jnp.float32
    )
    imag_sum = lax.dot_general(
        scaled_rows[1], piece[0], contract, preferred_element_type=jnp.float32
    )
    imag_sum = imag_sum - lax.dot_general(
        scaled_rows[0], piece[1], contract, preferred_element_type=jnp.float32
    )
    return jnp.stack([real_sum, imag_sum])


def solution(mesh):
    return jax.shard_map(
        local,
        mesh=mesh,
        in_specs=(P("val", "grid", None), P("cond", "grid", None), P(), P(), P()),
        out_specs=P(None, ("val", "grid"), "cond"),
        check_vma=False,
    )
```

profile of v0, /device:TPU:1, one launch (start us, length us, event | category | flops | bytes accessed | tf_op | source)
XLA Modules:
  0.0 897.4 jit_solution(11764834540841196857)
XLA Ops:
  6.5 128.8 %while.23 = (s32[]{:T(128)}, bf16[4,4,24,96,192]{4,2,1,0,3:T(8,128)(2,1)}, bf16[4,24,9216]{2,1,0:T(8,128)(2,1)}, bf16[4,24,9216]{2,1,0:T(8,128)(2,1)}, s32[]{:T(128)}) while((s32[]{:T(128)}, bf16[4,4,24,96,192]{4,2,1,0,3:T(8,128)(2,1)}, bf16[4,24,9216]{2,1,0:T(8,128)(2,1)}, bf16[4,24,9216]{2,1,0:T(8,128)(2,1)}, s32[]{:T(128)}) %tuple.68), condition=%wide.region_1.2_spmd, body=%wide.region_0.1_spmd.sunk | while | flops 1034855424 | bytes 90169952 | solution.py:110
  9.4 3.3 convert_element_type.200
  13.0 2.8 convolution_convert_fusion.4
  15.7 3.9 copy.96
  19.7 4.1 convolution_bitcast_fusion.4
  25.3 4.0 fusion.84
  29.3 4.4 pad_maximum_fusion.3
  33.8 4.9 copy_dynamic-update-slice_fusion.2
  41.6 3.3 convert_element_type.200
  47.9 3.9 copy.96
  51.8 4.1 convolution_bitcast_fusion.4
  57.5 4.0 fusion.84
  61.5 4.4 pad_maximum_fusion.3
  65.9 4.9 copy_dynamic-update-slice_fusion.2
  73.7 3.3 convert_element_type.200
  80.0 3.9 copy.96
  84.0 4.1 convolution_bitcast_fusion.4
  89.6 4.0 fusion.84
  93.6 4.4 pad_maximum_fusion.3
  98.0 5.1 copy_dynamic-update-slice_fusion.2
  106.0 3.3 convert_element_type.200
  112.3 3.9 copy.96
  116.2 4.1 convolution_bitcast_fusion.4
  121.9 4.0 fusion.84
  125.9 4.4 pad_maximum_fusion.3
  130.3 5.0 copy_dynamic-update-slice_fusion.2
  135.3 7.7 all-to-all-start
  144.5 204.8 %all-to-all-done = bf16[16,24,96,192]{3,1,0,2:T(8,128)(2,1)} async-done(((bf16[16,24,96,192]{3,1,0,2:T(8,128)(2,1)}), bf16[16,24,96,192]{3,1,0,2:T(8,128)(2,1)}, u32[]{:S(2)}, u32[]{:S(2)}) %all-to-all-start) | async-done | bytes 14155808 | tf_op jit(solution)/shard_map/all_to_all | solution.py:114
  349.3 35.3 %copy.48 = bf16[16,4,24,24,192]{4,3,2,1,0:T(8,128)(2,1)} copy(bf16[16,4,24,24,192]{4,2,0,3,1:T(8,128)(2,1)} %bitcast.10) | data formatting | bytes 28311552 | tf_op jit(solution)/shard_map/all_to_all | solution.py:114
  384.6 29.6 %reshape.152 = bf16[16,96,24,2,96]{4,3,2,1,0:T(2,128)(2,1)} reshape(bf16[16,4,24,24,192]{4,3,2,1,0:T(8,128)(2,1)} %copy.48) | data formatting | bytes 28311552 | tf_op jit(solution)/shard_map/reshape | solution.py:48
  414.2 60.5 %copy.73 = bf16[24,96,96,16,2]{2,4,3,1,0:T(2,128)(2,1)} copy(bf16[24,96,96,16,2]{1,4,0,2,3:T(2,128)(2,1)} %bitcast.126) | data formatting | bytes 28311552
  474.7 250.2 %while.24 = (s32[]{:T(128)}, bf16[12,2,512,16]{2,3,1,0:T(8,128)(2,1)S(1)}, s32[12,512]{1,0:T(8,128)}, s32[12,512]{1,0:T(8,128)S(1)}, bf16[2304,96,32]{1,2,0:T(8,128)(2,1)}, /*index=5*/f32[12,512]{1,0:T(8,128)}, s32[]{:T(128)}) while((s32[]{:T(128)}, bf16[12,2,512,16]{2,3,1,0:T(8,128)(2,1)S(1)}, s32[12,512]{1,0:T(8,128)}, ...), condition=%wide.region_3.4_spmd.clone, body=%wide.region_2.3_spmd.clone.sunk | while | flops 28887552 | bytes 29686932 | solution.py:86
  475.3 9.6 %gather_fusion = bf16[512,96,32]{1,2,0:T(8,128)(2,1)} fusion(bf16[2304,96,32]{1,2,0:T(8,128)(2,1)} %get-tuple-element.309, s32[1024]{0:T(1024)S(1)} %pad_clamp_fusion.2), kind=kCustom, calls=%fused_computation.clone.clone.1 | custom fusion | bytes 6293504 | tf_op jit(solution)/shard_map/while/body/eval_jaxpr/jit(_take)/gather | solution.py:68
  484.9 5.8 copy.98
  496.1 9.6 %gather_fusion = bf16[512,96,32]{1,2,0:T(8,128)(2,1)} fusion(bf16[2304,96,32]{1,2,0:T(8,128)(2,1)} %get-tuple-element.309, s32[1024]{0:T(1024)S(1)} %pad_clamp_fusion.2), kind=kCustom, calls=%fused_computation.clone.clone.1 | custom fusion | bytes 6293504 | tf_op jit(solution)/shard_map/while/body/eval_jaxpr/jit(_take)/gather | solution.py:68
  505.7 5.8 copy.98
  517.0 9.6 %gather_fusion = bf16[512,96,32]{1,2,0:T(8,128)(2,1)} fusion(bf16[2304,96,32]{1,2,0:T(8,128)(2,1)} %get-tuple-element.309, s32[1024]{0:T(1024)S(1)} %pad_clamp_fusion.2), kind=kCustom, calls=%fused_computation.clone.clone.1 | custom fusion | bytes 6293504 | tf_op jit(solution)/shard_map/while/body/eval_jaxpr/jit(_take)/gather | solution.py:68
  526.6 5.8 copy.98
  537.8 9.6 %gather_fusion = bf16[512,96,32]{1,2,0:T(8,128)(2,1)} fusion(bf16[2304,96,32]{1,2,0:T(8,128)(2,1)} %get-tuple-element.309, s32[1024]{0:T(1024)S(1)} %pad_clamp_fusion.2), kind=kCustom, calls=%fused_computation.clone.clone.1 | custom fusion | bytes 6293504 | tf_op jit(solution)/shard_map/while/body/eval_jaxpr/jit(_take)/gather | solution.py:68
  547.4 5.8 copy.98
  558.7 9.6 %gather_fusion = bf16[512,96,32]{1,2,0:T(8,128)(2,1)} fusion(bf16[2304,96,32]{1,2,0:T(8,128)(2,1)} %get-tuple-element.309, s32[1024]{0:T(1024)S(1)} %pad_clamp_fusion.2), kind=kCustom, calls=%fused_computation.clone.clone.1 | custom fusion | bytes 6293504 | tf_op jit(solution)/shard_map/while/body/eval_jaxpr/jit(_take)/gather | solution.py:68
  568.3 5.8 copy.98
  579.5 9.6 %gather_fusion = bf16[512,96,32]{1,2,0:T(8,128)(2,1)} fusion(bf16[2304,96,32]{1,2,0:T(8,128)(2,1)} %get-tuple-element.309, s32[1024]{0:T(1024)S(1)} %pad_clamp_fusion.2), kind=kCustom, calls=%fused_computation.clone.clone.1 | custom fusion | bytes 6293504 | tf_op jit(solution)/shard_map/while/body/eval_jaxpr/jit(_take)/gather | solution.py:68
  589.1 5.8 copy.98
  600.4 9.6 %gather_fusion = bf16[512,96,32]{1,2,0:T(8,128)(2,1)} fusion(bf16[2304,96,32]{1,2,0:T(8,128)(2,1)} %get-tuple-element.309, s32[1024]{0:T(1024)S(1)} %pad_clamp_fusion.2), kind=kCustom, calls=%fused_computation.clone.clone.1 | custom fusion | bytes 6293504 | tf_op jit(solution)/shard_map/while/body/eval_jaxpr/jit(_take)/gather | solution.py:68
  610.0 5.8 copy.98
  621.2 9.6 %gather_fusion = bf16[512,96,32]{1,2,0:T(8,128)(2,1)} fusion(bf16[2304,96,32]{1,2,0:T(8,128)(2,1)} %get-tuple-element.309, s32[1024]{0:T(1024)S(1)} %pad_clamp_fusion.2), kind=kCustom, calls=%fused_computation.clone.clone.1 | custom fusion | bytes 6293504 | tf_op jit(solution)/shard_map/while/body/eval_jaxpr/jit(_take)/gather | solution.py:68
  630.8 5.8 copy.98
  642.1 9.6 %gather_fusion = bf16[512,96,32]{1,2,0:T(8,128)(2,1)} fusion(bf16[2304,96,32]{1,2,0:T(8,128)(2,1)} %get-tuple-element.309, s32[1024]{0:T(1024)S(1)} %pad_clamp_fusion.2), kind=kCustom, calls=%fused_computation.clone.clone.1 | custom fusion | bytes 6293504 | tf_op jit(solution)/shard_map/while/body/eval_jaxpr/jit(_take)/gather | solution.py:68
  651.7 5.8 copy.98
  662.9 9.6 %gather_fusion = bf16[512,96,32]{1,2,0:T(8,128)(2,1)} fusion(bf16[2304,96,32]{1,2,0:T(8,128)(2,1)} %get-tuple-element.309, s32[1024]{0:T(1024)S(1)} %pad_clamp_fusion.2), kind=kCustom, calls=%fused_computation.clone.clone.1 | custom fusion | bytes 6293504 | tf_op jit(solution)/shard_map/while/body/eval_jaxpr/jit(_take)/gather | solution.py:68
  672.5 5.8 copy.98
  683.8 9.6 %gather_fusion = bf16[512,96,32]{1,2,0:T(8,128)(2,1)} fusion(bf16[2304,96,32]{1,2,0:T(8,128)(2,1)} %get-tuple-element.309, s32[1024]{0:T(1024)S(1)} %pad_clamp_fusion.2), kind=kCustom, calls=%fused_computation.clone.clone.1 | custom fusion | bytes 6293504 | tf_op jit(solution)/shard_map/while/body/eval_jaxpr/jit(_take)/gather | solution.py:68
  693.4 5.8 copy.98
  704.6 9.6 %gather_fusion = bf16[512,96,32]{1,2,0:T(8,128)(2,1)} fusion(bf16[2304,96,32]{1,2,0:T(8,128)(2,1)} %get-tuple-element.309, s32[1024]{0:T(1024)S(1)} %pad_clamp_fusion.2), kind=kCustom, calls=%fused_computation.clone.clone.1 | custom fusion | bytes 6293504 | tf_op jit(solution)/shard_map/while/body/eval_jaxpr/jit(_take)/gather | solution.py:68
  714.2 5.8 copy.98
  725.7 41.6 %all-reduce.2.cloned.1.call-done = bf16[2,16,6144]{2,1,0:T(8,128)(2,1)} async-done(((bf16[2,16,6144]{2,1,0:T(8,128)(2,1)}), bf16[2,16,6144]{2,1,0:T(8,128)(2,1)}) %all-reduce.2.cloned.1.call-update) | async-done | bytes 393232 | tf_op jit(solution)/shard_map/psum | solution.py:118
  770.0 6.1 copy.53
  776.1 3.3 reshape.183
  779.4 12.1 %all_to_all.33 = bf16[8,2,12288]{2,1,0:T(2,128)(2,1)} all-to-all(bf16[8,2,12288]{2,1,0:T(2,128)(2,1)S(1)} %reshape.183), channel_id=1, replica_groups=mesh['val'=4,'cond'=8,'grid'=4] {'cond'}, dimensions={0} | all-to-all | bytes 786432 | tf_op jit(solution)/shard_map/all_to_all | solution.py:137
  791.5 10.2 %reshape.184 = bf16[6144,2,16]{2,1,0:T(2,128)(2,1)S(1)} reshape(bf16[8,2,12288]{2,1,0:T(2,128)(2,1)} %all_to_all.33) | data formatting | bytes 786432
  801.7 4.8 copy.75
  806.9 51.1 %all-gather.3.cloned.1.call-done = bf16[2,512,1536]{2,1,0:T(8,128)(2,1)} async-done(((bf16[2,16,1536]{2,1,0:T(8,128)(2,1)}), bf16[2,512,1536]{2,1,0:T(8,128)(2,1)}) %all-gather.3.cloned.1.call-update) | async-done | bytes 3145744 | tf_op jit(solution)/shard_map/all_gather | solution.py:127
  859.4 25.5 %all-gather.5.cloned.1.call-done = bf16[2,512,768]{2,1,0:T(8,128)(2,1)} async-done(((bf16[2,128,768]{2,1,0:T(8,128)(2,1)}), bf16[2,512,768]{2,1,0:T(8,128)(2,1)}) %all-gather.5.cloned.1.call-update) | async-done | bytes 1572880 | tf_op jit(solution)/shard_map/all_gather | solution.py:139
  (254 shorter events, 104.0 us)
Async XLA Ops:
  19.7 4.1 copy-start
  51.8 4.1 copy-start
  84.0 4.1 copy-start
  116.2 4.1 copy-start
  135.3 7.8 copy-start.2
  135.3 213.9 %all-to-all-start = ((bf16[16,24,96,192]{3,1,0,2:T(8,128)(2,1)}), bf16[16,24,96,192]{3,1,0,2:T(8,128)(2,1)}, u32[]{:S(2)}, u32[]{:S(2)}) async-start(bf16[16,24,96,192]{3,1,0,2:T(8,128)(2,1)} %bitcast.127), calls=%async_computation | async-start | bytes 37748736 | tf_op jit(solution)/shard_map/all_to_all | solution.py:114
  143.1 624.3 %all-reduce.2.cloned.1.call-start = ((), (), s32[]{:S(2)}) async-start(), calls=%async_computation.2 | async-start | bytes 786432 | tf_op jit(solution)/shard_map/psum | solution.py:118
  474.7 0.6 copy-start.3
  491.2 4.3 copy-start.4
  495.5 0.6 copy-start.3
  512.0 4.3 copy-start.4
  516.4 0.6 copy-start.3
  532.9 4.3 copy-start.4
  537.2 0.6 copy-start.3
  553.7 4.3 copy-start.4
  558.1 0.6 copy-start.3
  574.6 4.3 copy-start.4
  578.9 0.6 copy-start.3
  595.4 4.3 copy-start.4
  599.8 0.6 copy-start.3
  616.3 4.3 copy-start.4
  620.6 0.6 copy-start.3
  637.1 4.3 copy-start.4
  641.5 0.6 copy-start.3
  658.0 4.3 copy-start.4
  662.3 0.6 copy-start.3
  678.8 4.3 copy-start.4
  683.2 0.6 copy-start.3
  699.7 4.3 copy-start.4
  704.0 0.6 copy-start.3
  720.5 4.3 copy-start.4
  725.7 132.3 %all-gather.3.cloned.1.call-start = ((), (), s32[]{:S(2)}) async-start(), calls=%async_computation.3 | async-start | bytes 3244032 | tf_op jit(solution)/shard_map/all_gather | solution.py:127
  770.0 114.9 %all-gather.5.cloned.1.call-start = ((), (), s32[]{:S(2)}) async-start(), calls=%async_computation.4 | async-start | bytes 1966080 | tf_op jit(solution)/shard_map/all_gather | solution.py:139
  791.5 15.0 %copy-start.5 = (f32[32]{0:T(128)S(1)}, f32[32]{0:T(128)}, u32[]{:S(2)}) copy-start(f32[32]{0:T(128)} %param.12) | copy-start | bytes 388
  791.5 15.1 %copy-start.6 = (f32[16]{0:T(128)S(1)}, f32[16]{0:T(128)}, u32[]{:S(2)}) copy-start(f32[16]{0:T(128)} %param.11) | copy-start | bytes 196
  884.8 3.4 copy-start.1
Sparse Core Ops, SparseCore 0:
  725.8 41.5 all-reduce.1
  770.1 87.8 all-gather.2
  859.7 25.0 all-gather.4
where the time goes:
time: 904 us; the launch traced here: 897 us
  local copies, waits for them, and re-layouts  415 us (46%)
  waiting for transfers between devices  323 us (36%)
  other arithmetic  77.3 us (9%)
  matrix products  47.5 us (5%)
  between operations  13.3 us (1%)
  blocking collectives  12.1 us (1%)
    all_to_all x1, waiting for transfers between devices, local(): lax.all_to_all(spectra, 'grid', split_axis=2, concat_axis=1, tiled=True)  205 us
    gather x24, local copies, waits for them, and re-layouts, one_block(): jnp.take(table_rows, picks, axis=0).reshape(block, NGRID, pair_total, 2)  184 us
    unnamed x11, local copies, waits for them, and re-layouts  73.9 us
    all_gather x1, waiting for transfers between devices, local(): lax.all_gather(grid_rows.reshape(2, pair_count, valence_groups * row_widt...  51.1 us
    psum x1, waiting for transfers between devices, local(): lax.psum(partial_values.astype(jnp.float32).astype(jnp.bfloat16), 'grid')  41.6 us
    all_to_all x1, local copies, waits for them, and re-layouts, local(): lax.all_to_all(spectra, 'grid', split_axis=2, concat_axis=1, tiled=True)  35.3 us
    reshape x1, local copies, waits for them, and re-layouts, line_pick(): split = pieces.reshape(pair_total, NGRID, local_rows, 2, NGRID)  29.6 us
    all_gather x1, waiting for transfers between devices, local(): piece = lax.all_gather(by_column, 'val', axis=1, tiled=True)  25.5 us
  transfers between devices with their start and end apart: 4, of which 4 were waited for; matrix products, arithmetic and copies ran while one was open for 3% of the time, Pallas kernels for 0%

commit v1 on v0

--- a/solution.py
+++ b/solution.py
@@ -124,12 +124,11 @@
     row_width = NG // (valence_groups * grid_groups)
     split_view = pair_values.reshape(2, pair_count, valence_groups, grid_groups, row_width)
     grid_rows = lax.dynamic_index_in_dim(split_view, lax.axis_index("grid"), 3, keepdims=False)
-    everything = lax.all_gather(
-        grid_rows.reshape(2, pair_count, valence_groups * row_width),
-        ("val", "cond"),
-        axis=1,
-        tiled=True,
-    )
+    block_2 = grid_rows.reshape(2, pair_count, valence_groups * row_width)
+    size = lax.axis_size(("val", "cond"))
+    parts = jnp.stack([block_2 for _ in range(size)])
+    parts = lax.all_to_all(parts, ("val", "cond"), split_axis=0, concat_axis=0)
+    everything = jnp.concatenate(parts, axis=1)
     row_values = lax.dynamic_slice_in_dim(
         everything, lax.axis_index("val") * row_width, row_width, 2
     )

time: 904 us -> 868 us (0.960)
  waiting for transfers between devices: 323 us -> 288 us
  starting transfers between devices: 7.85 us -> 21.6 us
  blocking collectives: 12.1 us -> 0 us
    all_gather x1 -> x0, waiting for transfers between devices: 51.1 us -> none  [local(): lax.all_gather(grid_rows.reshape(2, pair_count, valence_groups * row_widt...]
    all_to_all x0 -> x2, waiting for transfers between devices: none -> 41.1 us  [the longest x1 36.2 us: local(): parts = lax.all_to_all(parts, ('val', 'cond'), split_axis=0, concat_axis=0)]
    all_gather x1, waiting for transfers between devices: 25.5 us -> 0.02 us  [local(): piece = lax.all_gather(by_column, 'val', axis=1, tiled=True)]
    all_to_all x0 -> x2, starting transfers between devices: none -> 13.8 us  [the longest x1 8.76 us: local(): parts = lax.all_to_all(parts, ('val', 'cond'), split_axis=0, concat_axis=0)]
    all_to_all x1 -> x0, blocking collectives: 12.1 us -> none  [local(): lax.all_to_all(pair_values, 'cond', split_axis=2, concat_axis=1, tiled=True)]
  transfers between devices with their start and end apart: 4 -> 5, of which waited for: 4 -> 4; matrix products, arithmetic and copies ran while one was open for 3% -> 2% of each run, Pallas kernels for 0% -> 0%
where the time goes in v1:
time: 868 us; the launch traced here: 861 us
  local copies, waits for them, and re-layouts  414 us (48%)
  waiting for transfers between devices  288 us (33%)
  other arithmetic  76.2 us (9%)
  matrix products  47.6 us (5%)
  starting transfers between devices  21.6 us (2%)
  between operations  13.6 us (2%)
    all_to_all x1, waiting for transfers between devices, local(): lax.all_to_all(spectra, 'grid', split_axis=2, concat_axis=1, tiled=True)  205 us
    gather x24, local copies, waits for them, and re-layouts, one_block(): jnp.take(table_rows, picks, axis=0).reshape(block, NGRID, pair_total, 2)  185 us
    unnamed x11, local copies, waits for them, and re-layouts  67.7 us
    psum x1, waiting for transfers between devices, local(): lax.psum(partial_values.astype(jnp.float32).astype(jnp.bfloat16), 'grid')  41.7 us
    all_to_all x1, waiting for transfers between devices, local(): parts = lax.all_to_all(parts, ('val', 'cond'), split_axis=0, concat_axis=0)  36.2 us
    all_to_all x1, local copies, waits for them, and re-layouts, local(): lax.all_to_all(spectra, 'grid', split_axis=2, concat_axis=1, tiled=True)  35.4 us
    reshape x1, local copies, waits for them, and re-layouts, line_pick(): split = pieces.reshape(pair_total, NGRID, local_rows, 2, NGRID)  29.5 us
    dot_general x12, other arithmetic, one_block(): jnp.einsum('jx,jxp->jp', cos_pick, real_part, preferred_element_type=jnp....  24.1 us
  transfers between devices with their start and end apart: 5, of which 4 were waited for; matrix products, arithmetic and copies ran while one was open for 2% of the time, Pallas kernels for 0%

profile of v1, /device:TPU:1, one launch (start us, length us, event | category | flops | bytes accessed | tf_op | source)
XLA Modules:
  0.0 861.5 jit_solution(11609377670470530388)
XLA Ops:
  6.5 128.8 %while.23 = (s32[]{:T(128)}, bf16[4,4,24,96,192]{4,2,1,0,3:T(8,128)(2,1)}, bf16[4,24,9216]{2,1,0:T(8,128)(2,1)}, bf16[4,24,9216]{2,1,0:T(8,128)(2,1)}, s32[]{:T(128)}) while((s32[]{:T(128)}, bf16[4,4,24,96,192]{4,2,1,0,3:T(8,128)(2,1)}, bf16[4,24,9216]{2,1,0:T(8,128)(2,1)}, bf16[4,24,9216]{2,1,0:T(8,128)(2,1)}, s32[]{:T(128)}) %tuple.68), condition=%wide.region_1.2_spmd, body=%wide.region_0.1_spmd.sunk | while | flops 1034855424 | bytes 90169952 | solution.py:110
  9.4 3.3 convert_element_type.200
  15.7 4.0 copy.98
  19.7 4.1 convolution_bitcast_fusion.4
  25.3 4.0 fusion.84
  29.3 4.4 pad_maximum_fusion.3
  33.8 4.9 copy_dynamic-update-slice_fusion.2
  41.6 3.3 convert_element_type.200
  47.9 4.0 copy.98
  51.9 4.1 convolution_bitcast_fusion.4
  57.5 4.0 fusion.84
  61.5 4.4 pad_maximum_fusion.3
  66.0 5.0 copy_dynamic-update-slice_fusion.2
  73.8 3.3 convert_element_type.200
  80.1 4.0 copy.98
  84.1 4.1 convolution_bitcast_fusion.4
  89.7 4.0 fusion.84
  93.8 4.4 pad_maximum_fusion.3
  98.2 5.0 copy_dynamic-update-slice_fusion.2
  106.0 3.3 convert_element_type.200
  112.4 4.0 copy.98
  116.3 4.1 convolution_bitcast_fusion.4
  122.0 4.0 fusion.84
  126.0 4.4 pad_maximum_fusion.3
  130.4 4.9 copy_dynamic-update-slice_fusion.2
  135.3 7.7 all-to-all-start
  144.5 204.8 %all-to-all-done = bf16[16,24,96,192]{3,1,0,2:T(8,128)(2,1)} async-done(((bf16[16,24,96,192]{3,1,0,2:T(8,128)(2,1)}), bf16[16,24,96,192]{3,1,0,2:T(8,128)(2,1)}, u32[]{:S(2)}, u32[]{:S(2)}) %all-to-all-start) | async-done | bytes 14155808 | tf_op jit(solution)/shard_map/all_to_all | solution.py:114
  349.3 35.4 %copy.49 = bf16[16,4,24,24,192]{4,3,2,1,0:T(8,128)(2,1)} copy(bf16[16,4,24,24,192]{4,2,0,3,1:T(8,128)(2,1)} %bitcast.10) | data formatting | bytes 28311552 | tf_op jit(solution)/shard_map/all_to_all | solution.py:114
  384.7 29.5 %reshape.157 = bf16[16,96,24,2,96]{4,3,2,1,0:T(2,128)(2,1)} reshape(bf16[16,4,24,24,192]{4,3,2,1,0:T(8,128)(2,1)} %copy.49) | data formatting | bytes 28311552 | tf_op jit(solution)/shard_map/reshape | solution.py:48
  414.2 60.5 %copy.75 = bf16[24,96,96,16,2]{2,4,3,1,0:T(2,128)(2,1)} copy(bf16[24,96,96,16,2]{1,4,0,2,3:T(2,128)(2,1)} %bitcast.129) | data formatting | bytes 28311552
  474.7 250.3 %while.24 = (s32[]{:T(128)}, bf16[12,2,512,16]{2,3,1,0:T(8,128)(2,1)S(1)}, s32[12,512]{1,0:T(8,128)}, s32[12,512]{1,0:T(8,128)S(1)}, bf16[2304,96,32]{1,2,0:T(8,128)(2,1)}, /*index=5*/f32[12,512]{1,0:T(8,128)}, s32[]{:T(128)}) while((s32[]{:T(128)}, bf16[12,2,512,16]{2,3,1,0:T(8,128)(2,1)S(1)}, s32[12,512]{1,0:T(8,128)}, ...), condition=%wide.region_3.4_spmd.clone, body=%wide.region_2.3_spmd.clone.sunk | while | flops 28887552 | bytes 29686932 | solution.py:86
  475.3 9.6 %gather_fusion = bf16[512,96,32]{1,2,0:T(8,128)(2,1)} fusion(bf16[2304,96,32]{1,2,0:T(8,128)(2,1)} %get-tuple-element.309, s32[1024]{0:T(1024)S(1)} %pad_clamp_fusion.2), kind=kCustom, calls=%fused_computation.clone.clone.1 | custom fusion | bytes 6293504 | tf_op jit(solution)/shard_map/while/body/eval_jaxpr/jit(_take)/gather | solution.py:68
  484.9 5.8 copy.100
  496.2 9.6 %gather_fusion = bf16[512,96,32]{1,2,0:T(8,128)(2,1)} fusion(bf16[2304,96,32]{1,2,0:T(8,128)(2,1)} %get-tuple-element.309, s32[1024]{0:T(1024)S(1)} %pad_clamp_fusion.2), kind=kCustom, calls=%fused_computation.clone.clone.1 | custom fusion | bytes 6293504 | tf_op jit(solution)/shard_map/while/body/eval_jaxpr/jit(_take)/gather | solution.py:68
  505.8 5.8 copy.100
  517.1 9.6 %gather_fusion = bf16[512,96,32]{1,2,0:T(8,128)(2,1)} fusion(bf16[2304,96,32]{1,2,0:T(8,128)(2,1)} %get-tuple-element.309, s32[1024]{0:T(1024)S(1)} %pad_clamp_fusion.2), kind=kCustom, calls=%fused_computation.clone.clone.1 | custom fusion | bytes 6293504 | tf_op jit(solution)/shard_map/while/body/eval_jaxpr/jit(_take)/gather | solution.py:68
  526.7 5.8 copy.100
  537.9 9.6 %gather_fusion = bf16[512,96,32]{1,2,0:T(8,128)(2,1)} fusion(bf16[2304,96,32]{1,2,0:T(8,128)(2,1)} %get-tuple-element.309, s32[1024]{0:T(1024)S(1)} %pad_clamp_fusion.2), kind=kCustom, calls=%fused_computation.clone.clone.1 | custom fusion | bytes 6293504 | tf_op jit(solution)/shard_map/while/body/eval_jaxpr/jit(_take)/gather | solution.py:68
  547.5 5.8 copy.100
  558.8 9.6 %gather_fusion = bf16[512,96,32]{1,2,0:T(8,128)(2,1)} fusion(bf16[2304,96,32]{1,2,0:T(8,128)(2,1)} %get-tuple-element.309, s32[1024]{0:T(1024)S(1)} %pad_clamp_fusion.2), kind=kCustom, calls=%fused_computation.clone.clone.1 | custom fusion | bytes 6293504 | tf_op jit(solution)/shard_map/while/body/eval_jaxpr/jit(_take)/gather | solution.py:68
  568.4 5.8 copy.100
  579.6 9.6 %gather_fusion = bf16[512,96,32]{1,2,0:T(8,128)(2,1)} fusion(bf16[2304,96,32]{1,2,0:T(8,128)(2,1)} %get-tuple-element.309, s32[1024]{0:T(1024)S(1)} %pad_clamp_fusion.2), kind=kCustom, calls=%fused_computation.clone.clone.1 | custom fusion | bytes 6293504 | tf_op jit(solution)/shard_map/while/body/eval_jaxpr/jit(_take)/gather | solution.py:68
  589.2 5.8 copy.100
  600.5 9.6 %gather_fusion = bf16[512,96,32]{1,2,0:T(8,128)(2,1)} fusion(bf16[2304,96,32]{1,2,0:T(8,128)(2,1)} %get-tuple-element.309, s32[1024]{0:T(1024)S(1)} %pad_clamp_fusion.2), kind=kCustom, calls=%fused_computation.clone.clone.1 | custom fusion | bytes 6293504 | tf_op jit(solution)/shard_map/while/body/eval_jaxpr/jit(_take)/gather | solution.py:68
  610.1 5.8 copy.100
  621.4 9.6 %gather_fusion = bf16[512,96,32]{1,2,0:T(8,128)(2,1)} fusion(bf16[2304,96,32]{1,2,0:T(8,128)(2,1)} %get-tuple-element.309, s32[1024]{0:T(1024)S(1)} %pad_clamp_fusion.2), kind=kCustom, calls=%fused_computation.clone.clone.1 | custom fusion | bytes 6293504 | tf_op jit(solution)/shard_map/while/body/eval_jaxpr/jit(_take)/gather | solution.py:68
  631.0 5.8 copy.100
  642.2 9.6 %gather_fusion = bf16[512,96,32]{1,2,0:T(8,128)(2,1)} fusion(bf16[2304,96,32]{1,2,0:T(8,128)(2,1)} %get-tuple-element.309, s32[1024]{0:T(1024)S(1)} %pad_clamp_fusion.2), kind=kCustom, calls=%fused_computation.clone.clone.1 | custom fusion | bytes 6293504 | tf_op jit(solution)/shard_map/while/body/eval_jaxpr/jit(_take)/gather | solution.py:68
  651.8 5.8 copy.100
  663.1 9.6 %gather_fusion = bf16[512,96,32]{1,2,0:T(8,128)(2,1)} fusion(bf16[2304,96,32]{1,2,0:T(8,128)(2,1)} %get-tuple-element.309, s32[1024]{0:T(1024)S(1)} %pad_clamp_fusion.2), kind=kCustom, calls=%fused_computation.clone.clone.1 | custom fusion | bytes 6293504 | tf_op jit(solution)/shard_map/while/body/eval_jaxpr/jit(_take)/gather | solution.py:68
  672.7 5.8 copy.100
  684.0 9.6 %gather_fusion = bf16[512,96,32]{1,2,0:T(8,128)(2,1)} fusion(bf16[2304,96,32]{1,2,0:T(8,128)(2,1)} %get-tuple-element.309, s32[1024]{0:T(1024)S(1)} %pad_clamp_fusion.2), kind=kCustom, calls=%fused_computation.clone.clone.1 | custom fusion | bytes 6293504 | tf_op jit(solution)/shard_map/while/body/eval_jaxpr/jit(_take)/gather | solution.py:68
  693.6 5.8 copy.100
  704.8 9.6 %gather_fusion = bf16[512,96,32]{1,2,0:T(8,128)(2,1)} fusion(bf16[2304,96,32]{1,2,0:T(8,128)(2,1)} %get-tuple-element.309, s32[1024]{0:T(1024)S(1)} %pad_clamp_fusion.2), kind=kCustom, calls=%fused_computation.clone.clone.1 | custom fusion | bytes 6293504 | tf_op jit(solution)/shard_map/while/body/eval_jaxpr/jit(_take)/gather | solution.py:68
  714.4 5.8 copy.100
  725.9 41.7 %all-reduce.2.cloned.1.call-done = bf16[2,16,6144]{2,1,0:T(8,128)(2,1)} async-done(((bf16[2,16,6144]{2,1,0:T(8,128)(2,1)}), bf16[2,16,6144]{2,1,0:T(8,128)(2,1)}) %all-reduce.2.cloned.1.call-update) | async-done | bytes 393232 | tf_op jit(solution)/shard_map/psum | solution.py:118
  767.5 6.1 copy.55
  773.6 3.9 reshape.189
  777.5 5.1 all-to-all-start.2
  784.5 4.9 all-to-all-done.2
  791.4 8.8 %all-to-all-start.1 = ((bf16[32,2,16,1536]{3,2,1,0:T(8,128)(2,1)}), bf16[32,2,16,1536]{3,2,1,0:T(8,128)(2,1)S(1)}, u32[]{:S(2)}, u32[]{:S(2)}) async-start(bf16[32,2,16,1536]{3,2,1,0:T(8,128)(2,1)} %stack.21), calls=%async_computation.1 | async-start | bytes 6291456 | tf_op jit(solution)/shard_map/all_to_all | solution.py:130
  800.3 3.3 reshape.190
  803.6 8.0 copy.77
  812.0 36.2 %all-to-all-done.1 = bf16[32,2,16,1536]{3,2,1,0:T(8,128)(2,1)S(1)} async-done(((bf16[32,2,16,1536]{3,2,1,0:T(8,128)(2,1)}), bf16[32,2,16,1536]{3,2,1,0:T(8,128)(2,1)S(1)}, u32[]{:S(2)}, u32[]{:S(2)}) %all-to-all-start.1) | async-done | bytes 3145760 | tf_op jit(solution)/shard_map/all_to_all | solution.py:130
  (256 shorter events, 107.2 us)
Async XLA Ops:
  19.7 4.1 copy-start
  51.9 4.1 copy-start
  84.1 4.1 copy-start
  116.3 4.1 copy-start
  135.3 7.8 copy-start.2
  135.3 214.0 %all-to-all-start = ((bf16[16,24,96,192]{3,1,0,2:T(8,128)(2,1)}), bf16[16,24,96,192]{3,1,0,2:T(8,128)(2,1)}, u32[]{:S(2)}, u32[]{:S(2)}) async-start(bf16[16,24,96,192]{3,1,0,2:T(8,128)(2,1)} %bitcast.130), calls=%async_computation | async-start | bytes 37748736 | tf_op jit(solution)/shard_map/all_to_all | solution.py:114
  143.0 624.5 %all-reduce.2.cloned.1.call-start = ((), (), s32[]{:S(2)}) async-start(), calls=%async_computation.3 | async-start | bytes 786432 | tf_op jit(solution)/shard_map/psum | solution.py:118
  474.7 0.6 copy-start.3
  491.2 4.3 copy-start.4
  495.6 0.6 copy-start.3
  512.1 4.3 copy-start.4
  516.5 0.6 copy-start.3
  533.0 4.3 copy-start.4
  537.3 0.6 copy-start.3
  553.8 4.3 copy-start.4
  558.2 0.6 copy-start.3
  574.7 4.3 copy-start.4
  579.0 0.6 copy-start.3
  595.5 4.3 copy-start.4
  599.9 0.6 copy-start.3
  616.4 4.3 copy-start.4
  620.8 0.6 copy-start.3
  637.3 4.3 copy-start.4
  641.6 0.6 copy-start.3
  658.1 4.3 copy-start.4
  662.5 0.6 copy-start.3
  679.0 4.3 copy-start.4
  683.4 0.6 copy-start.3
  699.9 4.3 copy-start.4
  704.2 0.6 copy-start.3
  720.7 4.3 copy-start.4
  777.5 11.9 %all-to-all-start.2 = ((bf16[8,2,12288]{2,1,0:T(2,128)(2,1)}), bf16[8,2,12288]{2,1,0:T(2,128)(2,1)S(1)}, u32[]{:S(2)}, u32[]{:S(2)}) async-start(bf16[8,2,12288]{2,1,0:T(2,128)(2,1)} %reshape.189), calls=%async_computation.2 | async-start | bytes 786432 | tf_op jit(solution)/shard_map/all_to_all | solution.py:136
  791.4 56.7 %all-to-all-start.1 = ((bf16[32,2,16,1536]{3,2,1,0:T(8,128)(2,1)}), bf16[32,2,16,1536]{3,2,1,0:T(8,128)(2,1)S(1)}, u32[]{:S(2)}, u32[]{:S(2)}) async-start(bf16[32,2,16,1536]{3,2,1,0:T(8,128)(2,1)} %stack.21), calls=%async_computation.1 | async-start | bytes 6291456 | tf_op jit(solution)/shard_map/all_to_all | solution.py:130
  800.2 11.4 %copy-start.5 = (f32[32]{0:T(128)S(1)}, f32[32]{0:T(128)}, u32[]{:S(2)}) copy-start(f32[32]{0:T(128)} %param.12) | copy-start | bytes 388
  800.2 11.4 %copy-start.6 = (f32[16]{0:T(128)S(1)}, f32[16]{0:T(128)}, u32[]{:S(2)}) copy-start(f32[16]{0:T(128)} %param.11) | copy-start | bytes 196
  800.2 48.4 %all-gather.2.cloned.1.call-start = ((), (), s32[]{:S(2)}) async-start(), calls=%async_computation.4 | async-start | bytes 1966080 | tf_op jit(solution)/shard_map/all_gather | solution.py:138
  848.7 3.4 copy-start.1
Sparse Core Ops, SparseCore 0:
  726.0 41.4 all-reduce.1
  811.7 32.7 all-gather.1
